TPU v7x, 256 devices: a whole 4x4x8 slice. The times are simulated.
256 devices in a mesh: row: 32 (over y, x, core), col: 8 (over z).
Axes of the slice: x: 4, y: 4, z: 8, core: 2. Of those that a mesh axis runs over, the one named last changes fastest.
Arguments:
- panel: float32 [24576, 256], P('row', 'col'), may hold values from -6 to 6
- trailing: float32 [24576, 12032], P('row', 'col'), may hold values from -6 to 6
Outputs:
- projections: float32 [12032, 256], P('col')
- remainder: float32 [24576, 12032], P('row', 'col')
All inputs are finite; a program needn't handle non-finite values.
Results may differ from a plain program's by a relative error of at most 0.000075.
Values sent between devices are 32-bit elements; how exact they have to be, the bound alone decides.
A program may use at most 64 MiB of HBM per device.

v0:
```python
import jax
import jax.numpy as jnp
from jax import lax
from jax.sharding import PartitionSpec as P


def cross_rows(left, right):
    return lax.dot_general(
        left,
        right,
        (((0,), (0,)), ((), ())),
        precision=lax.Precision.HIGHEST,
        preferred_element_type=jnp.float32,
    )


def solve_right(lower_factor, terms):
    return jax.scipy.linalg.solve_triangular(lower_factor, terms.T, lower=True).T


def per_device(panel, trailing):
    panel_full = lax.all_gather(panel, "col", axis=1, tiled=True)
    panel_gram = lax.psum(cross_rows(panel_full, panel_full), "row")
    lower_factor = jnp.linalg.cholesky(panel_gram)
    orthonormal = solve_right(lower_factor, panel_full)
    cross_terms = lax.psum(cross_rows(trailing, panel_full), "row")
    projections = solve_right(lower_factor, cross_terms)
    update = lax.dot_general(
        orthonormal,
        projections,
        (((1,), (1,)), ((), ())),
        precision=lax.Precision.HIGHEST,
        preferred_element_type=jnp.float32,
    )
    remainder = trailing - update
    return (projections, remainder)


def solution(mesh):
    return jax.shard_map(
        per_device,
        mesh=mesh,
        in_specs=(P("row", "col"), P("row", "col")),
        out_specs=(P("col", None), P("row", "col")),
        check_vma=False,
    )
```

profile of v0, /device:TPU:6, one launch (start us, length us, event | category | flops | bytes accessed | tf_op | source)
XLA Modules:
  0.0 242.3 jit_solution(3756788934562251100)
XLA Ops:
  7.2 0.0 all-reduce.4.cloned.1.call-start
  7.2 30.0 %all_gather.3 = f32[768,256]{0,1:T(8,128)S(1)} all-gather(f32[768,32]{0,1:T(8,128)} %param.2), channel_id=1, replica_groups=mesh['row'=32,'col'=8] {'col'}, dimensions={1}, use_global_device_ids=true | all-gather | bytes 884736 | tf_op jit(solution)/shard_map/all_gather | solution.py:22
  37.2 1.5 fusion.18
  38.8 7.3 %fusion.19 = f32[256,1504]{0,1:T(8,128)} fusion(f32[768,256]{0,1:T(8,128)S(1)} %all_gather.3, f32[768,1504]{0,1:T(8,128)} %param.3), kind=kOutput, calls=%fused_computation.41 | convolution fusion | flops 3548381184 | bytes 6946816 | tf_op jit(solution)/shard_map/dot_general | solution.py:8
  46.1 0.0 all-reduce.4.cloned.1.call-update
  46.1 116.7 %all-reduce.4.cloned.1.call-done = (f32[256,1504]{0,1:T(8,128)}, f32[256,256]{0,1:T(8,128)}) async-done(((f32[256,1504]{0,1:T(8,128)}, f32[256,256]{0,1:T(8,128)}), (f32[256,1504]{0,1:T(8,128)}, f32[256,256]{0,1:T(8,128)})) %all-reduce.4.cloned.1.call-update) | async-done | bytes 1802256 | tf_op jit(solution)/shard_map/psum | solution.py:26
  162.8 1.1 copy.5
  163.9 0.0 slice-start
  163.9 1.0 fusion.8
  165.0 11.7 %cholesky.50 = f32[128,128]{1,0:T(8,128)S(1)} custom-call(f32[128,128]{1,0:T(8,128)S(1)} %cholesky.118), custom_call_target="Cholesky" | custom-call | tf_op jit(solution)/shard_map/jit(cholesky)/cholesky | solution.py:24
  176.7 9.8 %custom-call.18 = f32[1,128,128]{1,2,0:T(8,128)S(1)} custom-call(f32[1,128,128]{2,1,0:T(8,128)S(1)} %get-tuple-element.25), custom_call_target="InvertDiagBlocksLowerTriangular" | custom-call | tf_op jit(solution)/shard_map/jit(cholesky)/cholesky | solution.py:24
  186.6 0.2 constant_dynamic-update-slice_fusion.1
  186.8 0.3 convolution_subtract_fusion.3
  187.0 11.9 %cholesky.105 = f32[128,128]{1,0:T(8,128)S(1)} custom-call(f32[128,128]{1,0:T(8,128)S(1)} %convolution_subtract_fusion.3), custom_call_target="Cholesky" | custom-call | tf_op jit(solution)/shard_map/jit(cholesky)/cholesky | solution.py:24
  199.0 0.6 compare_reduce_fusion
  200.9 0.1 triangular_solve.72
  201.0 4.0 %while.1 = (s32[]{:T(128)}, f32[256,256]{1,0:T(8,128)S(1)}, s32[2,2]{1,0:T(2,128)S(1)}, f32[2,128,128]{2,1,0:T(8,128)S(1)}, s32[]{:T(128)}) while((s32[]{:T(128)}, f32[256,256]{1,0:T(8,128)S(1)}, s32[2,2]{1,0:T(2,128)S(1)}, f32[2,128,128]{2,1,0:T(8,128)S(1)}, s32[]{:T(128)}) %tuple.27), condition=%wide.while_cond, body=%wide.while_body.sunk | while | flops 2 | bytes 131181 | solution.py:18
  201.0 0.6 fusion.31
  201.6 1.4 bitcast_dynamic-update-slice_fusion.2
  203.0 0.6 fusion.31
  203.6 1.4 bitcast_dynamic-update-slice_fusion.2
  205.0 0.0 copy-start
  205.0 19.7 %custom-call.19 = f32[2,128,128]{1,2,0:T(8,128)S(1)} custom-call(f32[2,128,128]{2,1,0:T(8,128)S(1)} %get-tuple-element.9), custom_call_target="InvertDiagBlocksLowerTriangular" | custom-call | tf_op jit(solution)/shard_map/jit(_solve_triangular)/triangular_solve | solution.py:18
  224.7 0.5 fusion.6
  225.2 0.5 convolution_subtract_fusion.2
  225.7 0.5 fusion.12
  226.2 0.0 copy-done
  226.2 0.0 slice-start.1
  226.2 0.8 fusion.4
  227.0 0.8 convolution_subtract_fusion.1
  227.8 0.8 fusion.13
  228.6 1.2 fusion
  229.8 0.0 slice-done
  229.8 0.0 slice-done.1
  229.8 5.6 %convolution_subtract_fusion = f32[768,1504]{0,1:T(8,128)} fusion(f32[768,1504]{0,1:T(8,128)S(1)} %bitcast.45, f32[128,1504]{0,1:T(8,128)S(1)} %fusion.13, f32[128,1504]{0,1:T(8,128)S(1)} %fusion.4, f32[128,768]{1,0:T(8,128)S(1)} %fusion.12, f32[128,768]{1,0:T(8,128)S(1)} %fusion.6), kind=kOutput, calls=%fused_computation.2 | convolution fusion | flops 3550117888 | bytes 11567104 | tf_op jit(solution)/shard_map/dot_general | solution.py:28
  (10 shorter events, 0.1 us)
Async XLA Ops:
  7.2 155.7 %all-reduce.4.cloned.1.call-start = ((), (), s32[]{:S(2)}) async-start(), calls=%async_computation | async-start | bytes 3604480 | tf_op jit(solution)/shard_map/psum | solution.py:26
  163.9 65.9 %slice-start = ((s8[4620288]{0:T(1024)(128)(4,1)}), s8[425984]{0:T(1024)(128)(4,1)S(1)}, s32[]{:S(2)}) async-start(s8[4620288]{0:T(1024)(128)(4,1)} %bitcast.44), calls=%async_computation.1 | async-start | bytes 851968
  205.0 21.2 %copy-start = (f32[256,1504]{0,1:T(8,128)S(1)}, f32[256,1504]{0,1:T(8,128)}, u32[]{:S(2)}) copy-start(f32[256,1504]{0,1:T(8,128)} %get-tuple-element.18) | copy-start | bytes 4620292
  226.2 3.6 %slice-start.1 = ((s8[4620288]{0:T(1024)(128)(4,1)}), s8[4194304]{0:T(1024)(128)(4,1)S(1)}, s32[]{:S(2)}) async-start(s8[4620288]{0:T(1024)(128)(4,1)} %bitcast.44), calls=%async_computation.2 | async-start | bytes 8388608
Sparse Core Ops, SparseCore 0:
  46.2 116.5 all-reduce.3
where the time goes:
time: 243 us; the launch traced here: 242 us
  waiting for transfers between devices  117 us (48%)
  other arithmetic  56.1 us (23%)
  blocking collectives  30 us (12%)
  matrix products  18.8 us (8%)
  between operations  15.5 us (6%)
  local copies, waits for them, and re-layouts  5.15 us (2%)
    psum x1, waiting for transfers between devices, per_device(): cross_terms = lax.psum(cross_rows(trailing, panel_full), 'row')  117 us
    another operation x6, other arithmetic, per_device(): lower_factor = jnp.linalg.cholesky(panel_gram)  34.1 us
    all_gather x1, blocking collectives, per_device(): panel_full = lax.all_gather(panel, 'col', axis=1, tiled=True)  30 us
    another operation x3, other arithmetic, solve_right(): jax.scipy.linalg.solve_triangular(lower_factor, terms.T, lower=True)  19.7 us
    dot_general x2, matrix products, cross_rows(): lax.dot_general(left, right, (((0,), (0,)), ((), ())), precision=lax.Prec...  8.83 us
    dot_general x1, matrix products, per_device(): lax.dot_general(orthonormal, projections, (((1,), (1,)), ((), ())), preci...  5.64 us
  transfers between devices with their start and end apart: 1, of which 1 were waited for; matrix products, arithmetic and copies ran while one was open for 0% of the time, Pallas kernels for 0%

commit v1 on v0

--- a/solution.py
+++ b/solution.py
@@ -2,6 +2,12 @@
 import jax.numpy as jnp
 from jax import lax
 from jax.sharding import PartitionSpec as P
+from jax.lax import all_gather
+
+
+def find_trails(unit, comm_axis):
+    lower = jnp.sum(all_gather(unit, comm_axis), 0)
+    return lower
 
 
 def cross_rows(left, right):
@@ -23,7 +29,7 @@
     panel_gram = lax.psum(cross_rows(panel_full, panel_full), "row")
     lower_factor = jnp.linalg.cholesky(panel_gram)
     orthonormal = solve_right(lower_factor, panel_full)
-    cross_terms = lax.psum(cross_rows(trailing, panel_full), "row")
+    cross_terms = find_trails(cross_rows(trailing, panel_full), "row")
     projections = solve_right(lower_factor, cross_terms)
     update = lax.dot_general(
         orthonormal,

time: 243 us -> 351 us (1.44)
  waiting for transfers between devices: 117 us -> 204 us
  other arithmetic: 56.1 us -> 74 us
    all_gather x0 -> x1, waiting for transfers between devices: none -> 99 us  [find_trails(): lower = jnp.sum(all_gather(unit, comm_axis), 0)]
    reduce_sum x0 -> x1, other arithmetic: none -> 17.9 us  [find_trails(): lower = jnp.sum(all_gather(unit, comm_axis), 0)]
    psum x1, waiting for transfers between devices: 117 us -> 105 us  [per_device(): panel_gram = lax.psum(cross_rows(panel_full, panel_full), 'row')]
  transfers between devices with their start and end apart: 1 -> 2, of which waited for: 1 -> 2; matrix products, arithmetic and copies ran while one was open for 0% -> 20% of each run, Pallas kernels for 0% -> 0%
where the time goes in v1:
time: 351 us; the launch traced here: 349 us
  waiting for transfers between devices  204 us (58%)
  other arithmetic  74 us (21%)
  blocking collectives  30 us (9%)
  matrix products  20.4 us (6%)
  between operations  15.4 us (4%)
  local copies, waits for them, and re-layouts  4.93 us (1%)
    psum x1, waiting for transfers between devices, per_device(): panel_gram = lax.psum(cross_rows(panel_full, panel_full), 'row')  105 us
    all_gather x1, waiting for transfers between devices, find_trails(): lower = jnp.sum(all_gather(unit, comm_axis), 0)  99 us
    another operation x6, other arithmetic, per_device(): lower_factor = jnp.linalg.cholesky(panel_gram)  34.1 us
    all_gather x1, blocking collectives, per_device(): panel_full = lax.all_gather(panel, 'col', axis=1, tiled=True)  30 us
    another operation x3, other arithmetic, solve_right(): jax.scipy.linalg.solve_triangular(lower_factor, terms.T, lower=True)  19.7 us
    reduce_sum x1, other arithmetic, find_trails(): lower = jnp.sum(all_gather(unit, comm_axis), 0)  17.9 us
    dot_general x2, matrix products, cross_rows(): lax.dot_general(left, right, (((0,), (0,)), ((), ())), precision=lax.Prec...  8.79 us
    dot_general x1, matrix products, per_device(): lax.dot_general(orthonormal, projections, (((1,), (1,)), ((), ())), preci...  7.3 us
  transfers between devices with their start and end apart: 2, of which 2 were waited for; matrix products, arithmetic and copies ran while one was open for 20% of the time, Pallas kernels for 0%

profile of v1, /device:TPU:6, one launch (start us, length us, event | category | flops | bytes accessed | tf_op | source)
XLA Modules:
  0.0 349.1 jit_solution(424194414774949908)
XLA Ops:
  7.2 0.0 all-reduce.3.cloned.1.call-start
  7.2 30.0 %all_gather.9 = f32[768,256]{0,1:T(8,128)S(1)} all-gather(f32[768,32]{0,1:T(8,128)} %param.2), channel_id=1, replica_groups=mesh['row'=32,'col'=8] {'col'}, dimensions={1}, use_global_device_ids=true | all-gather | bytes 884736 | tf_op jit(solution)/shard_map/all_gather | solution.py:28
  37.2 1.5 fusion.18
  38.8 0.0 all-reduce.3.cloned.1.call-update
  38.8 0.0 all-gather.3.cloned.1.call-start
  38.8 7.3 %fusion.19 = f32[1504,256]{1,0:T(8,128)} fusion(f32[768,1504]{0,1:T(8,128)} %param.3, f32[768,256]{0,1:T(8,128)S(1)} %all_gather.9), kind=kOutput, calls=%fused_computation.41 | convolution fusion | flops 3548381184 | bytes 6946816 | tf_op jit(solution)/shard_map/dot_general | solution.py:14
  46.1 0.0 all-gather.3.cloned.1.call-update
  46.1 105.2 %all-reduce.3.cloned.1.call-done = f32[256,256]{0,1:T(8,128)} async-done(((f32[256,256]{0,1:T(8,128)}), f32[256,256]{0,1:T(8,128)}) %all-reduce.3.cloned.1.call-update) | async-done | bytes 262160 | tf_op jit(solution)/shard_map/psum | solution.py:29
  151.3 1.1 copy.5
  152.4 1.0 fusion.8
  153.4 11.7 %cholesky.50 = f32[128,128]{1,0:T(8,128)S(1)} custom-call(f32[128,128]{1,0:T(8,128)S(1)} %cholesky.118), custom_call_target="Cholesky" | custom-call | tf_op jit(solution)/shard_map/jit(cholesky)/cholesky | solution.py:30
  165.2 9.8 %custom-call.18 = f32[1,128,128]{1,2,0:T(8,128)S(1)} custom-call(f32[1,128,128]{2,1,0:T(8,128)S(1)} %get-tuple-element.23), custom_call_target="InvertDiagBlocksLowerTriangular" | custom-call | tf_op jit(solution)/shard_map/jit(cholesky)/cholesky | solution.py:30
  175.0 0.2 constant_dynamic-update-slice_fusion.1
  175.2 0.3 convolution_subtract_fusion.3
  175.5 11.9 %cholesky.105 = f32[128,128]{1,0:T(8,128)S(1)} custom-call(f32[128,128]{1,0:T(8,128)S(1)} %convolution_subtract_fusion.3), custom_call_target="Cholesky" | custom-call | tf_op jit(solution)/shard_map/jit(cholesky)/cholesky | solution.py:30
  187.4 0.6 compare_reduce_fusion
  189.3 0.1 triangular_solve.72
  189.4 3.8 %while.1 = (s32[]{:T(128)}, f32[256,256]{1,0:T(8,128)S(1)}, s32[2,2]{1,0:T(2,128)S(1)}, f32[2,128,128]{2,1,0:T(8,128)S(1)}, s32[]{:T(128)}) while((s32[]{:T(128)}, f32[256,256]{1,0:T(8,128)S(1)}, s32[2,2]{1,0:T(2,128)S(1)}, f32[2,128,128]{2,1,0:T(8,128)S(1)}, s32[]{:T(128)}) %tuple.27), condition=%wide.while_cond, body=%wide.while_body.sunk | while | flops 2 | bytes 131189 | solution.py:24
  189.4 0.6 fusion.31
  189.9 1.3 bitcast_dynamic-update-slice_fusion.2
  191.3 0.6 fusion.31
  191.9 1.3 bitcast_dynamic-update-slice_fusion.2
  193.1 19.7 %custom-call.19 = f32[2,128,128]{1,2,0:T(8,128)S(1)} custom-call(f32[2,128,128]{2,1,0:T(8,128)S(1)} %get-tuple-element.9), custom_call_target="InvertDiagBlocksLowerTriangular" | custom-call | tf_op jit(solution)/shard_map/jit(_solve_triangular)/triangular_solve | solution.py:24
  212.8 0.5 fusion.6
  213.4 0.5 convolution_subtract_fusion.2
  213.8 0.5 fusion.12
  214.4 99.0 %all-gather.3.cloned.1.call-done = f32[48128,256]{1,0:T(8,128)} async-done(((f32[1504,256]{1,0:T(8,128)}), f32[48128,256]{1,0:T(8,128)}) %all-gather.3.cloned.1.call-update) | async-done | bytes 49283088 | tf_op jit(solution)/shard_map/all_gather | solution.py:9
  313.4 17.9 %reduce_sum.9 = f32[1504,256]{1,0:T(8,128)S(1)} reduce(f32[32,1504,256]{2,1,0:T(8,128)} %bitcast.44, f32[]{:T(128)} %constant.85.clone.1), dimensions={0}, to_apply=%region_5.6 | reduce | flops 11935744 | bytes 50823172 | tf_op jit(solution)/shard_map/reduce_sum | solution.py:9
  331.3 0.8 fusion.4
  332.1 0.8 convolution_subtract_fusion.1
  332.9 0.8 fusion.13
  333.7 1.2 fusion
  334.9 7.3 %convolution_subtract_fusion = f32[768,1504]{0,1:T(8,128)} fusion(f32[768,1504]{0,1:T(8,128)} %param.3, f32[128,1504]{0,1:T(8,128)S(1)} %fusion.13, f32[128,1504]{0,1:T(8,128)S(1)} %fusion.4, f32[128,768]{1,0:T(8,128)S(1)} %fusion.12, f32[128,768]{1,0:T(8,128)S(1)} %fusion.6), kind=kOutput, calls=%fused_computation.2 | convolution fusion | flops 3550117888 | bytes 11567104 | tf_op jit(solution)/shard_map/dot_general | solution.py:34
  (9 shorter events, 0.1 us)
Async XLA Ops:
  7.2 144.2 %all-reduce.3.cloned.1.call-start = ((), (), s32[]{:S(2)}) async-start(), calls=%async_computation | async-start | bytes 524288 | tf_op jit(solution)/shard_map/psum | solution.py:29
  38.8 274.6 %all-gather.3.cloned.1.call-start = ((), (), s32[]{:S(2)}) async-start(), calls=%async_computation.1 | async-start | bytes 50823168 | tf_op jit(solution)/shard_map/all_gather | solution.py:9
Sparse Core Ops, SparseCore 0:
  38.9 112.3 all-reduce.2
  154.4 158.9 all-gather.2
